TPU v7x, 256 devices: a whole 4x4x8 slice. The times are simulated.
256 devices in a mesh: batch: 64 (over y, z, core), feat: 4 (over x).
Axes of the slice: x: 4, y: 4, z: 8, core: 2. Of those that a mesh axis runs over, the one named last changes fastest.
Arguments:
- tables: bfloat16 [4, 128, 2048, 192], P('feat', 'batch'), may hold values from -3 to 3
- bag_ids: int32 [4, 128, 4, 8192], P('feat', 'batch'), may hold values from 0 to 2047
- bag_lengths: int32 [4, 128, 8192], P('feat', 'batch'), may hold values from 1 to 4
- pair_groups: int32 [16, 2], replicated, may hold values from 0 to 15
- compress: bfloat16 [16, 32, 8], P('feat'), may hold values from -1 to 1
- w_hidden: bfloat16 [16, 32, 8, 4096], P('feat'), may hold values from -0.09375 to 0.09375
- hidden_bias: float32 [4096], replicated, may hold values from -4 to 4
- norm_gain: float32 [4096], P('feat'), may hold values from 0.1 to 1.9
Outputs:
- interacted: bfloat16 [8192, 4096], P('batch', 'feat')
Inputs may be any that keep to these rules, and one draw needn't show every extreme that they name: `bag_lengths`: ids at slots from a bag's length on are ignored.
All inputs are finite; a program needn't handle non-finite values.
Results may differ from a plain program's by a relative error of at most 0.0052.
Values may be sent and summed in bfloat16 or wider, within the bound.
A program may use at most 128 MiB of HBM per device.

v0:
```python
import jax
import jax.numpy as jnp
from jax import lax
from jax.sharding import PartitionSpec as P


def take_rows(table_one, ids_one):
    return jnp.take(table_one, ids_one, axis=0)


def select_groups(source, pair_list, group_size):
    offsets = jnp.arange(group_size, dtype=jnp.int32)
    wanted = pair_list[:, :, None] * group_size + offsets[None, None, :]
    shape_out = (pair_list.shape[0], 2, group_size, source.shape[1], source.shape[2])
    return jnp.take(source, wanted.reshape(-1), axis=0).reshape(shape_out)


def squeeze_pairs(chosen, weights):
    row_blocks = chosen[:, 0]
    col_blocks = chosen[:, 1]
    gram_scale = float(chosen.shape[4]) ** (-0.5)
    gram_blocks = (
        jnp.einsum("qfbd,qgbd->qbfg", row_blocks, col_blocks, preferred_element_type=jnp.float32)
        * gram_scale
    )
    squeezed = jnp.einsum(
        "qbfg,qgk->bqfk", gram_blocks, weights.astype(jnp.float32), precision=lax.Precision.HIGHEST
    )
    return squeezed.astype(jnp.bfloat16)


def body(tables, bag_ids, bag_lengths, pair_groups, compress, w_hidden, hidden_bias, norm_gain):
    own_tables = tables[0]
    own_ids = bag_ids[0]
    own_lengths = bag_lengths[0]
    slot_count = own_ids.shape[1]
    pooled_sum = jnp.zeros((own_ids.shape[0], own_ids.shape[2], own_tables.shape[2]), jnp.float32)
    for slot in range(slot_count):
        looked = jax.vmap(take_rows)(own_tables, own_ids[:, slot, :])
        live = (own_lengths > slot)[:, :, None]
        pooled_sum = pooled_sum + jnp.where(live, looked.astype(jnp.float32), 0.0)
    pooled = pooled_sum.astype(jnp.bfloat16)
    feature_tile = lax.all_to_all(pooled, "batch", split_axis=1, concat_axis=0, tiled=True)
    samples = feature_tile.shape[1]
    pair_count = compress.shape[0]
    group_size = compress.shape[1]
    first_pair = lax.axis_index("feat") * pair_count
    local_pairs = lax.dynamic_slice_in_dim(pair_groups, first_pair, pair_count, 0)
    everything = lax.all_gather(feature_tile, "feat", axis=0, tiled=True)
    squeezed = squeeze_pairs(select_groups(everything, local_pairs, group_size), compress)
    squeezed = squeezed.reshape(samples, -1)
    w_flat = w_hidden.reshape(-1, w_hidden.shape[3])
    hid_local = norm_gain.shape[0]
    hid_total = hid_local * lax.axis_size("feat")
    own_start = lax.axis_index("feat") * hid_local
    hidden = lax.psum_scatter(
        lax.dot_general(
            w_flat, squeezed, (((0,), (1,)), ((), ())), preferred_element_type=jnp.float32
        ),
        "feat",
        scatter_dimension=0,
        tiled=True,
    )
    local_bias = lax.dynamic_slice_in_dim(hidden_bias, own_start, hid_local, 0)
    hidden = hidden + local_bias[:, None]
    row_sum, row_squares = lax.psum(
        (jnp.sum(hidden, axis=0), jnp.sum(hidden * hidden, axis=0)), "feat"
    )
    row_mean = row_sum / hid_total
    spread = row_squares / hid_total - row_mean * row_mean
    normed = (hidden - row_mean[None, :]) * lax.rsqrt(spread + 1e-05)[None, :] * norm_gain[:, None]
    return jax.nn.silu(normed).T.astype(jnp.bfloat16)


def solution(mesh):
    in_specs = (
        P("feat", "batch", None, None),
        P("feat", "batch", None, None),
        P("feat", "batch", None),
        P(),
        P("feat", None, None),
        P("feat", None, None, None),
        P(),
        P("feat"),
    )
    out_specs = P("batch", "feat")
    return jax.shard_map(body, mesh=mesh, in_specs=in_specs, out_specs=out_specs, check_vma=False)
```

profile of v0, /device:TPU:8, one launch (start us, length us, event | category | flops | bytes accessed | tf_op | source)
XLA Modules:
  0.0 1334.6 jit_solution(744671372483452733)
XLA Ops:
  6.5 0.0 copy-start
  6.5 0.0 all-gather.2.cloned.1.call-start
  6.5 1.8 fusion.15
  8.3 0.2 fusion.12
  8.5 0.2 compare_and_fusion.2
  8.7 0.2 fusion.10
  8.9 0.2 compare_and_fusion
  9.1 2.7 copy.38
  11.9 161.2 %gather_fusion.3 = bf16[16384,192]{1,0:T(8,128)(2,1)} fusion(bf16[2,2048,192]{2,1,0:T(8,128)(2,1)S(1)} %bitcast.104, s32[16384]{0:T(1024)S(1)} %bitcast.108), kind=kCustom, calls=%fused_computation.2.clone | custom fusion | bytes 12713984 | tf_op jit(solution)/shard_map/vmap(jit(_take))/gather | solution.py:8
  173.1 161.2 %gather_fusion.4 = bf16[16384,192]{1,0:T(8,128)(2,1)} fusion(bf16[2,2048,192]{2,1,0:T(8,128)(2,1)S(1)} %bitcast.105, s32[16384]{0:T(1024)S(1)} %bitcast.109), kind=kCustom, calls=%fused_computation.3.clone | custom fusion | bytes 12713984 | tf_op jit(solution)/shard_map/vmap(jit(_take))/gather | solution.py:8
  334.3 161.1 %gather_fusion.1 = bf16[16384,192]{1,0:T(8,128)(2,1)} fusion(bf16[2,2048,192]{2,1,0:T(8,128)(2,1)S(1)} %bitcast.106, s32[16384]{0:T(1024)S(1)} %bitcast.111), kind=kCustom, calls=%fused_computation.clone | custom fusion | bytes 12713984 | tf_op jit(solution)/shard_map/vmap(jit(_take))/gather | solution.py:8
  495.4 0.0 copy-start.1
  495.4 161.2 %gather_fusion.2 = bf16[16384,192]{1,0:T(8,128)(2,1)} fusion(bf16[2,2048,192]{2,1,0:T(8,128)(2,1)S(1)} %bitcast.107, s32[16384]{0:T(1024)S(1)} %bitcast.110), kind=kCustom, calls=%fused_computation.1.clone | custom fusion | bytes 12713984 | tf_op jit(solution)/shard_map/vmap(jit(_take))/gather | solution.py:8
  656.6 1.7 copy.37
  658.3 1.7 copy.41
  660.1 1.7 copy.44
  661.8 2.2 copy.47
  664.0 0.0 copy-done.1
  664.0 0.1 compare_bitcast_fusion.3
  664.2 2.2 copy.36
  666.3 2.1 copy.40
  668.5 2.1 copy.43
  670.6 2.2 copy.46
  672.8 79.1 %add_convert_fusion = bf16[2,8192,192]{2,0,1:T(2,128)(2,1)S(1)} fusion(pred[2,8192]{0,1:T(8,128)(4,1)} %copy.46, pred[2,8192]{0,1:T(8,128)(4,1)} %copy.43, pred[2,8192]{0,1:T(8,128)(4,1)} %copy.40, pred[2,8192]{0,1:T(8,128)(4,1)} %copy.36, pred[2,8192]{0,1:T(8,128)(4,1)S(1)} %copy.37, pred[2,8192]{0,1:T(8,128)(4,1)S(1)} %copy.41, ...), kind=kLoop, calls=%fused_computation.5 | loop fusion | flops 50331648 | bytes 31588352 | tf_op jit(solution)/shard_map/convert_element_type | solution.py:42
  751.8 196.1 %all_to_all.18 = bf16[2,8192,192]{2,0,1:T(2,128)(2,1)} all-to-all(bf16[2,8192,192]{2,0,1:T(2,128)(2,1)S(1)} %add_convert_fusion), channel_id=1, replica_groups=mesh['batch'=64,'feat'=4] {'batch'}, dimensions={1} | all-to-all | bytes 12582912 | tf_op jit(solution)/shard_map/all_to_all | solution.py:43
  948.0 0.0 copy-start.3
  948.0 20.4 %copy.56 = bf16[2,64,128,192]{2,3,0,1:T(8,128)(2,1)} copy(bf16[2,64,128,192]{3,0,2,1:T(2,128)(2,1)} %bitcast.113) | data formatting | bytes 12582912 | tf_op jit(solution)/shard_map/all_to_all | solution.py:43
  968.4 0.0 all-gather.2.cloned.1.call-update
  968.4 0.2 reduce-scatter.2.cloned.1.call-start
  968.6 0.0 copy-done.3
  968.6 0.1 dynamic-slice_multiply_fusion
  968.7 0.1 copy.34
  968.8 0.1 iota_add_fusion
  968.9 0.1 add.103
  969.0 0.1 compare_and_fusion.4
  969.1 224.3 %all-gather.2.cloned.1.call-done = bf16[512,128,192]{1,2,0:T(8,128)(2,1)} async-done(((bf16[128,128,192]{1,2,0:T(8,128)(2,1)}), bf16[512,128,192]{1,2,0:T(8,128)(2,1)}) %all-gather.2.cloned.1.call-update) | async-done | bytes 25165840 | tf_op jit(solution)/shard_map/all_gather | solution.py:49
  1193.3 18.8 %gather_fusion = bf16[256,128,192]{1,2,0:T(8,128)(2,1)} fusion(bf16[512,128,192]{1,2,0:T(8,128)(2,1)} %all-gather.2.cloned.1.call-done, s32[1024]{0:T(1024)S(1)} %pad_clamp_fusion), kind=kCustom, calls=%fused_computation.4 | custom fusion | bytes 25166848 | tf_op jit(solution)/shard_map/jit(_take)/gather | solution.py:15
  1212.1 27.1 %copy.51 = bf16[4,2,32,128,192]{4,2,3,0,1:T(8,128)(2,1)} copy(bf16[4,2,32,128,192]{3,4,2,1,0:T(8,128)(2,1)} %bitcast.112) | data formatting | bytes 25165824 | tf_op jit(solution)/shard_map/jit(_take)/gather | solution.py:15
  1239.3 14.1 %broadcast_select_fusion.4 = bf16[4,2,32,128,192]{4,2,3,0,1:T(8,128)(2,1)} fusion(bf16[4,2,32,128,192]{4,2,3,0,1:T(8,128)(2,1)} %copy.51, pred[4,2,32]{2,0,1:T(4,128)(4,1)S(1)} %copy.35), kind=kLoop, calls=%fused_computation.10 | loop fusion | flops 6291456 | bytes 25166080 | tf_op jit(solution)/shard_map/jit(_take)/select_n | solution.py:15
  1253.4 11.3 broadcast_multiply_fusion
  1264.7 0.0 copy-done
  1264.7 11.9 fusion.6
  1276.6 0.0 copy-start.2
  1276.6 6.1 convolution_bitcast_fusion
  1282.7 0.0 reduce-scatter.2.cloned.1.call-update
  1282.7 0.7 dynamic_slice.7
  1283.4 32.5 %reduce-scatter.2.cloned.1.call-done = f32[1024,128]{0,1:T(8,128)} async-done(((f32[4096,128]{0,1:T(8,128)}), f32[1024,128]{0,1:T(8,128)}) %reduce-scatter.2.cloned.1.call-update) | async-done | bytes 524304 | tf_op jit(solution)/shard_map/reduce_scatter | solution.py:56
  1315.9 1.2 add_reduce_fusion
  1317.1 8.6 all-reduce
  1325.7 0.0 copy-done.2
  1325.7 2.0 fusion.9
  (8 shorter events, 0.1 us)
Async XLA Ops:
  6.5 1258.2 %copy-start = (bf16[4,32,8]{1,2,0:T(8,128)(2,1)S(1)}, bf16[4,32,8]{1,2,0:T(8,128)(2,1)}, u32[]{:S(2)}) copy-start(bf16[4,32,8]{1,2,0:T(8,128)(2,1)} %param.14) | copy-start | bytes 6148
  6.5 1186.8 %all-gather.2.cloned.1.call-start = ((), (), s32[]{:S(2)}) async-start(), calls=%async_computation.2 | async-start | bytes 31457280 | tf_op jit(solution)/shard_map/all_gather | solution.py:49
  495.4 168.6 %copy-start.1 = (s32[1,2,8192]{2,1,0:T(2,128)S(1)}, s32[1,2,8192]{2,1,0:T(2,128)}, u32[]{:S(2)}) copy-start(s32[1,2,8192]{2,1,0:T(2,128)} %param.12) | copy-start | bytes 196612
  948.0 20.6 %copy-start.3 = (s32[16,2]{0,1:T(2,128)S(1)}, s32[16,2]{0,1:T(2,128)}, u32[]{:S(2)}) copy-start(s32[16,2]{0,1:T(2,128)} %param.13) | copy-start | bytes 388
  968.4 347.6 %reduce-scatter.2.cloned.1.call-start = ((), (), s32[]{:S(2)}) async-start(), calls=%async_computation.3 | async-start | bytes 2621440 | tf_op jit(solution)/shard_map/reduce_scatter | solution.py:56
  1276.6 49.1 %copy-start.2 = (f32[1024]{0:T(1024)S(1)}, f32[1024]{0:T(1024)}, u32[]{:S(2)}) copy-start(f32[1024]{0:T(1024)} %param.17) | copy-start | bytes 12292
Sparse Core Ops, SparseCore 0:
  968.5 224.7 all-gather.1
  1282.8 33.0 reduce-scatter.1
where the time goes:
time: 1340 us; the launch traced here: 1330 us
  local copies, waits for them, and re-layouts  732 us (55%)
  waiting for transfers between devices  257 us (19%)
  blocking collectives  205 us (15%)
  other arithmetic  97.5 us (7%)
  matrix products  29.3 us (2%)
  between operations  13.6 us (1%)
    gather x4, local copies, waits for them, and re-layouts, take_rows(): return jnp.take(table_one, ids_one, axis=0)  645 us
    all_gather x1, waiting for transfers between devices, body(): everything = lax.all_gather(feature_tile, 'feat', axis=0, tiled=True)  224 us
    all_to_all x1, blocking collectives, body(): lax.all_to_all(pooled, 'batch', split_axis=1, concat_axis=0, tiled=True)  196 us
    convert_element_type x1, other arithmetic, body(): pooled = pooled_sum.astype(jnp.bfloat16)  79.1 us
    gather x2, local copies, waits for them, and re-layouts, select_groups(): return jnp.take(source, wanted.reshape(-1), axis=0).reshape(shape_out)  45.9 us
    reduce_scatter x1, waiting for transfers between devices, body(): lax.psum_scatter(lax.dot_general(w_flat, squeezed, (((0,), (1,)), ((), ()...  32.5 us
  transfers between devices with their start and end apart: 2, of which 2 were waited for; matrix products, arithmetic and copies ran while one was open for 0% of the time, Pallas kernels for 0%

commit v1 on v0

--- a/solution.py
+++ b/solution.py
@@ -46,7 +46,15 @@
     group_size = compress.shape[1]
     first_pair = lax.axis_index("feat") * pair_count
     local_pairs = lax.dynamic_slice_in_dim(pair_groups, first_pair, pair_count, 0)
-    everything = lax.all_gather(feature_tile, "feat", axis=0, tiled=True)
+    everything = jnp.concatenate(
+        lax.all_to_all(
+            jnp.stack(tuple((feature_tile for _ in range(lax.axis_size("feat"))))),
+            "feat",
+            split_axis=0,
+            concat_axis=0,
+        ),
+        axis=0,
+    )
     squeezed = squeeze_pairs(select_groups(everything, local_pairs, group_size), compress)
     squeezed = squeezed.reshape(samples, -1)
     w_flat = w_hidden.reshape(-1, w_hidden.shape[3])

time: 1340 us -> 1410 us (1.052)
  waiting for transfers between devices: 257 us -> 302 us
  local copies, waits for them, and re-layouts: 732 us -> 748 us
    all_to_all x0 -> x1, waiting for transfers between devices: none -> 274 us  [body(): lax.all_to_all(jnp.stack(tuple((feature_tile for _ in range(lax.axis_size...]
    all_gather x1 -> x0, waiting for transfers between devices: 224 us -> none  [body(): everything = lax.all_gather(feature_tile, 'feat', axis=0, tiled=True)]
where the time goes in v1:
time: 1410 us; the launch traced here: 1400 us
  local copies, waits for them, and re-layouts  748 us (53%)
  waiting for transfers between devices  302 us (21%)
  blocking collectives  205 us (15%)
  other arithmetic  97.5 us (7%)
  matrix products  29.3 us (2%)
    gather x4, local copies, waits for them, and re-layouts, take_rows(): return jnp.take(table_one, ids_one, axis=0)  649 us
    all_to_all x1, waiting for transfers between devices, body(): lax.all_to_all(jnp.stack(tuple((feature_tile for _ in range(lax.axis_size...  274 us
    all_to_all x1, blocking collectives, body(): lax.all_to_all(pooled, 'batch', split_axis=1, concat_axis=0, tiled=True)  196 us
    convert_element_type x1, other arithmetic, body(): pooled = pooled_sum.astype(jnp.bfloat16)  79.1 us
    gather x2, local copies, waits for them, and re-layouts, select_groups(): return jnp.take(source, wanted.reshape(-1), axis=0).reshape(shape_out)  45.9 us
  transfers between devices with their start and end apart: 2, of which 2 were waited for; matrix products, arithmetic and copies ran while one was open for 0% of the time, Pallas kernels for 0%

profile of v1, /device:TPU:8, one launch (start us, length us, event | category | flops | bytes accessed | tf_op | source)
XLA Modules:
  0.0 1403.2 jit_solution(12250282406190803289)
XLA Ops:
  6.5 0.0 copy-start
  6.5 1.6 fusion.15
  8.1 0.2 fusion.12
  8.3 0.2 compare_and_fusion.2
  8.5 0.2 fusion.10
  8.7 0.2 compare_and_fusion
  8.9 2.7 copy.51
  11.7 162.3 %gather_fusion.3 = bf16[16384,192]{1,0:T(8,128)(2,1)} fusion(bf16[2,2048,192]{2,1,0:T(8,128)(2,1)S(1)} %bitcast.105, s32[16384]{0:T(1024)S(1)} %bitcast.109), kind=kCustom, calls=%fused_computation.2.clone | custom fusion | bytes 12713984 | tf_op jit(solution)/shard_map/vmap(jit(_take))/gather | solution.py:8
  174.0 162.3 %gather_fusion.4 = bf16[16384,192]{1,0:T(8,128)(2,1)} fusion(bf16[2,2048,192]{2,1,0:T(8,128)(2,1)S(1)} %bitcast.106, s32[16384]{0:T(1024)S(1)} %bitcast.110), kind=kCustom, calls=%fused_computation.3.clone | custom fusion | bytes 12713984 | tf_op jit(solution)/shard_map/vmap(jit(_take))/gather | solution.py:8
  336.3 162.3 %gather_fusion.1 = bf16[16384,192]{1,0:T(8,128)(2,1)} fusion(bf16[2,2048,192]{2,1,0:T(8,128)(2,1)S(1)} %bitcast.107, s32[16384]{0:T(1024)S(1)} %bitcast.112), kind=kCustom, calls=%fused_computation.clone | custom fusion | bytes 12713984 | tf_op jit(solution)/shard_map/vmap(jit(_take))/gather | solution.py:8
  498.6 0.0 copy-start.1
  498.6 162.3 %gather_fusion.2 = bf16[16384,192]{1,0:T(8,128)(2,1)} fusion(bf16[2,2048,192]{2,1,0:T(8,128)(2,1)S(1)} %bitcast.108, s32[16384]{0:T(1024)S(1)} %bitcast.111), kind=kCustom, calls=%fused_computation.1.clone | custom fusion | bytes 12713984 | tf_op jit(solution)/shard_map/vmap(jit(_take))/gather | solution.py:8
  660.8 1.7 copy.50
  662.5 1.7 copy.54
  664.3 1.7 copy.57
  666.0 2.2 copy.60
  668.2 0.0 copy-done.1
  668.2 0.1 compare_bitcast_fusion.3
  668.4 2.2 copy.49
  670.5 2.1 copy.53
  672.7 2.1 copy.56
  674.8 2.2 copy.59
  677.0 79.1 %add_convert_fusion = bf16[2,8192,192]{2,0,1:T(2,128)(2,1)S(1)} fusion(pred[2,8192]{0,1:T(8,128)(4,1)} %copy.59, pred[2,8192]{0,1:T(8,128)(4,1)} %copy.56, pred[2,8192]{0,1:T(8,128)(4,1)} %copy.53, pred[2,8192]{0,1:T(8,128)(4,1)} %copy.49, pred[2,8192]{0,1:T(8,128)(4,1)S(1)} %copy.50, pred[2,8192]{0,1:T(8,128)(4,1)S(1)} %copy.54, ...), kind=kLoop, calls=%fused_computation.5 | loop fusion | flops 50331648 | bytes 31588352 | tf_op jit(solution)/shard_map/convert_element_type | solution.py:42
  756.0 196.1 %all_to_all.20 = bf16[2,8192,192]{2,0,1:T(2,128)(2,1)} all-to-all(bf16[2,8192,192]{2,0,1:T(2,128)(2,1)S(1)} %add_convert_fusion), channel_id=1, replica_groups=mesh['batch'=64,'feat'=4] {'batch'}, dimensions={1} | all-to-all | bytes 12582912 | tf_op jit(solution)/shard_map/all_to_all | solution.py:43
  952.2 20.4 %copy.69 = bf16[2,64,128,192]{2,3,0,1:T(8,128)(2,1)} copy(bf16[2,64,128,192]{3,0,2,1:T(2,128)(2,1)} %bitcast.114) | data formatting | bytes 12582912 | tf_op jit(solution)/shard_map/all_to_all | solution.py:43
  972.6 11.1 stack.10
  983.7 0.0 copy-start.3
  983.7 8.7 all-to-all-start.1
  992.5 0.0 reduce-scatter.2.cloned.1.call-start
  992.5 0.0 copy-done.3
  992.5 0.1 dynamic-slice_multiply_fusion
  992.6 0.1 copy.47
  992.7 0.1 iota_add_fusion
  992.8 0.1 add.103
  992.9 0.1 compare_and_fusion.4
  993.0 273.8 %all-to-all-done.1 = bf16[4,128,128,192]{2,3,1,0:T(8,128)(2,1)} async-done(((bf16[4,128,128,192]{2,3,1,0:T(8,128)(2,1)}), bf16[4,128,128,192]{2,3,1,0:T(8,128)(2,1)}, u32[]{:S(2)}, u32[]{:S(2)}) %all-to-all-start.1) | async-done | bytes 25165856 | tf_op jit(solution)/shard_map/all_to_all | solution.py:50
  1266.7 18.8 %gather_fusion = bf16[256,128,192]{1,2,0:T(8,128)(2,1)} fusion(bf16[512,128,192]{1,2,0:T(8,128)(2,1)} %bitcast.18, s32[1024]{0:T(1024)S(1)} %pad_clamp_fusion), kind=kCustom, calls=%fused_computation.4 | custom fusion | bytes 25166848 | tf_op jit(solution)/shard_map/jit(_take)/gather | solution.py:15
  1285.5 27.1 %copy.64 = bf16[4,2,32,128,192]{4,2,3,0,1:T(8,128)(2,1)} copy(bf16[4,2,32,128,192]{3,4,2,1,0:T(8,128)(2,1)} %bitcast.113) | data formatting | bytes 25165824 | tf_op jit(solution)/shard_map/jit(_take)/gather | solution.py:15
  1312.6 14.1 %broadcast_select_fusion.4 = bf16[4,2,32,128,192]{4,2,3,0,1:T(8,128)(2,1)} fusion(bf16[4,2,32,128,192]{4,2,3,0,1:T(8,128)(2,1)} %copy.64, pred[4,2,32]{2,0,1:T(4,128)(4,1)S(1)} %copy.48), kind=kLoop, calls=%fused_computation.10 | loop fusion | flops 6291456 | bytes 25166080 | tf_op jit(solution)/shard_map/jit(_take)/select_n | solution.py:15
  1326.8 11.4 broadcast_multiply_fusion
  1338.1 0.0 copy-done
  1338.1 11.9 fusion.6
  1350.0 0.0 copy-start.2
  1350.0 6.1 convolution_bitcast_fusion
  1356.1 0.0 reduce-scatter.2.cloned.1.call-update
  1356.1 0.7 dynamic_slice.7
  1356.8 27.7 %reduce-scatter.2.cloned.1.call-done = f32[1024,128]{0,1:T(8,128)} async-done(((f32[4096,128]{0,1:T(8,128)}), f32[1024,128]{0,1:T(8,128)}) %reduce-scatter.2.cloned.1.call-update) | async-done | bytes 524304 | tf_op jit(solution)/shard_map/reduce_scatter | solution.py:64
  1384.5 1.2 add_reduce_fusion
  1385.7 8.6 all-reduce
  1394.3 0.0 copy-done.2
  1394.3 2.0 fusion.9
  (8 shorter events, 0.1 us)
Async XLA Ops:
  6.5 1331.6 %copy-start = (bf16[4,32,8]{1,2,0:T(8,128)(2,1)S(1)}, bf16[4,32,8]{1,2,0:T(8,128)(2,1)}, u32[]{:S(2)}) copy-start(bf16[4,32,8]{1,2,0:T(8,128)(2,1)} %param.14) | copy-start | bytes 6148
  498.6 169.7 %copy-start.1 = (s32[1,2,8192]{2,1,0:T(2,128)S(1)}, s32[1,2,8192]{2,1,0:T(2,128)}, u32[]{:S(2)}) copy-start(s32[1,2,8192]{2,1,0:T(2,128)} %param.12) | copy-start | bytes 196612
  983.7 8.8 copy-start.3
  983.7 283.0 %all-to-all-start.1 = ((bf16[4,128,128,192]{2,3,1,0:T(8,128)(2,1)}), bf16[4,128,128,192]{2,3,1,0:T(8,128)(2,1)}, u32[]{:S(2)}, u32[]{:S(2)}) async-start(bf16[4,128,128,192]{2,3,1,0:T(8,128)(2,1)} %stack.10), calls=%async_computation.1 | async-start | bytes 50331648 | tf_op jit(solution)/shard_map/all_to_all | solution.py:50
  992.5 392.1 %reduce-scatter.2.cloned.1.call-start = ((), (), s32[]{:S(2)}) async-start(), calls=%async_computation.3 | async-start | bytes 2621440 | tf_op jit(solution)/shard_map/reduce_scatter | solution.py:64
  1350.0 44.3 %copy-start.2 = (f32[1024]{0:T(1024)S(1)}, f32[1024]{0:T(1024)}, u32[]{:S(2)}) copy-start(f32[1024]{0:T(1024)} %param.17) | copy-start | bytes 12292
Sparse Core Ops, SparseCore 0:
  1356.2 28.2 reduce-scatter.1
